TPU v7x, 32 devices: a whole 2x2x4 slice. The times are simulated.
32 devices in a mesh: dp: 8 (over z, core), tensor: 4 (over y, x).
Axes of the slice: x: 2, y: 2, z: 4, core: 2. Of those that a mesh axis runs over, the one named last changes fastest.
Arguments:
- tokens: bfloat16 [24576, 1024], P('dp'), may hold values from -6 to 6
- lengths: int32 [24], P('dp'), may hold values from 512 to 1024, as said below
- routes: int32 [24576, 1], P('dp'), may hold values from 0 to 7
- fill_order: int32 [8, 3072], P('dp'), may hold values from 0 to 3071, each once within a row
- norm_gain: float32 [1024], replicated, may hold values from 0.1 to 1.9
- norm_bias: float32 [1024], replicated, may hold values from -3 to 3
- qkv_weight: bfloat16 [1024, 16, 192], P(None, 'tensor'), may hold values from -0.1875 to 0.1875
- out_weight: bfloat16 [16, 64, 1024], P('tensor'), may hold values from -0.75 to 0.75
- centroids: bfloat16 [8, 1024], P('dp'), may hold values from -0.125 to 0.125
- expert_in: bfloat16 [8, 2, 1024, 4096], P('dp', None, None, 'tensor'), may hold values from -0.1875 to 0.1875
- expert_out: bfloat16 [8, 2, 4096, 1024], P('dp', None, 'tensor'), may hold values from -0.09375 to 0.09375
- cotangent: bfloat16 [24576, 1024], P('dp'), may hold values from -6 to 6
Outputs:
- output: bfloat16 [24576, 1024], P('dp')
- grad_tokens: bfloat16 [24576, 1024], P('dp')
- grad_norm_gain: float32 [1024], P('tensor')
- grad_norm_bias: float32 [1024], P('tensor')
- grad_qkv_weight: float32 [1024, 16, 192], P(None, 'tensor')
- grad_out_weight: float32 [16, 64, 1024], P('tensor')
- grad_centroids: float32 [8, 1024], P('dp')
- grad_expert_in: float32 [8, 2, 1024, 4096], P('dp', None, None, 'tensor')
- grad_expert_out: float32 [8, 2, 4096, 1024], P('dp', None, 'tensor')
Inputs may be any that keep to these rules, and one draw needn't show every extreme that they name: `lengths`: valid tokens of each sequence; one sequence has exactly 1024 and one exactly 512.
All inputs are finite; a program needn't handle non-finite values.
Results may differ from a plain program's by a relative error of at most 0.015.
Values may be sent and summed in bfloat16 or wider, within the bound.
A program may use at most 448 MiB of HBM per device.

v0:
```python
import math
import jax
import jax.numpy as jnp
from jax import lax
from jax.sharding import PartitionSpec as P

EPSILON = 1e-05
HIGHEST = lax.Precision.HIGHEST
F32 = jnp.float32
BF16 = jnp.bfloat16


class Grid:

    def __init__(self, size):
        inner = int(math.isqrt(size))
        while size % inner:
            inner -= 1
        self.size = size
        self.parts = {"x": inner, "y": size // inner}

    def _pairs(self, axis, shift):
        wide, tall = (self.parts["x"], self.parts["y"])
        pairs = []
        for row in range(tall):
            for col in range(wide):
                if axis == "x":
                    other = row * wide + (col + shift) % wide
                else:
                    other = (row + shift) % tall * wide + col
                pairs.append((other, row * wide + col))
        return pairs

    def fetch(self, value, axis, shift=1):
        return lax.ppermute(value, "tensor", self._pairs(axis, shift))

    def gather_list(self, value, axis):
        return [value] + [self.fetch(value, axis, s) for s in range(1, self.parts[axis])]

    def scatter_list(self, parts, axis):
        total = parts[0]
        for s in range(1, self.parts[axis]):
            total = total + self.fetch(parts[s].astype(BF16), axis, -s).astype(F32)
        return total


def gather_rows(grid, value):
    if grid.size != 4:
        return lax.all_gather(value, "tensor", axis=0, tiled=False)
    half = value.shape[0] // 2
    me = lax.axis_index("tensor")
    first, second = (value[:half], value[half:])
    first_x = grid.fetch(first, "x")
    second_y = grid.fetch(second, "y")
    first_y = grid.fetch(first, "y")
    second_x = grid.fetch(second, "x")
    first_xy = grid.fetch(first_x, "y")
    second_xy = grid.fetch(second_y, "x")
    out = jnp.zeros((4,) + value.shape, value.dtype)
    out = lax.dynamic_update_slice(out, value[None], (me, 0, 0))
    for other, top, bottom in (
        (1, first_x, second_x),
        (2, first_y, second_y),
        (3, first_xy, second_xy),
    ):
        place = jnp.bitwise_xor(me, other)
        out = lax.dynamic_update_slice(out, top[None], (place, 0, 0))
        out = lax.dynamic_update_slice(out, bottom[None], (place, half, 0))
    return out


def scatter_rows(grid, term):
    size, rows, width = term.shape
    if size != 4:
        return lax.psum_scatter(
            term.astype(BF16), "tensor", scatter_dimension=0, tiled=False
        ).astype(F32)
    me = lax.axis_index("tensor")
    half = width // 2

    def pick(other, low):
        place = jnp.bitwise_xor(me, other)
        return lax.dynamic_slice(term, (place, 0, low), (1, rows, half))[0]

    totals = []
    for low, near, far, near_axis, far_axis in ((0, 1, 2, "x", "y"), (half, 2, 1, "y", "x")):
        got_far = grid.fetch(pick(3, low).astype(BF16), near_axis)
        got_own = grid.fetch(pick(near, low).astype(BF16), near_axis)
        onward = pick(far, low).astype(F32) + got_far.astype(F32)
        got = grid.fetch(onward.astype(BF16), far_axis)
        totals.append(pick(0, low).astype(F32) + got_own.astype(F32) + got.astype(F32))
    return jnp.concatenate(totals, axis=1)


def gelu_pair(pre):
    cdf = 0.5 * (1.0 + lax.erf(pre * 2.0 ** (-0.5)))
    density = jnp.exp(-0.5 * pre * pre) * (2.0 * math.pi) ** (-0.5)
    return ((pre * cdf).astype(BF16), (cdf + pre * density).astype(BF16))


def plan_slots(routes, order, lengths, seq_len, experts, capacity, padded):
    count = routes.shape[0]
    seq_count = lengths.shape[0]
    places = jnp.arange(count, dtype=jnp.int32)
    limits = jnp.broadcast_to(lengths[:, None], (seq_count, seq_len)).reshape(count)
    is_valid = places % seq_len < limits
    order_row = order.reshape(count)
    route_sorted = routes.reshape(count)[order_row]
    valid_sorted = is_valid[order_row]
    matches = (
        (route_sorted[:, None] == jnp.arange(experts, dtype=jnp.int32)[None, :])
        & valid_sorted[:, None]
    ).astype(jnp.int32)
    before = jnp.cumsum(matches, axis=0) - matches
    rank_sorted = jnp.sum(before * matches, axis=1)
    kept_sorted = valid_sorted & (rank_sorted < capacity)
    slot_sorted = jnp.where(kept_sorted, route_sorted * padded + rank_sorted, experts * padded)
    slot_token = (
        jnp.full((experts * padded + 1,), count, jnp.int32)
        .at[slot_sorted]
        .set(order_row)[: experts * padded]
    )
    token_slot = jnp.zeros((count,), jnp.int32).at[order_row].set(slot_sorted)
    return (slot_token, token_slot)


def dot(a, b, contract):
    return lax.dot_general(a, b, (contract, ((), ())), preferred_element_type=F32)


def body(
    tokens,
    lengths,
    routes,
    fill_order,
    norm_gain,
    norm_bias,
    qkv_weight,
    out_weight,
    centroids,
    expert_in,
    expert_out,
    cotangent,
):
    tok_count, model_width = tokens.shape
    seq_count = lengths.shape[0]
    seq_len = tok_count // seq_count
    heads_here = qkv_weight.shape[1]
    head_size = out_weight.shape[1]
    experts = lax.axis_size("dp")
    shards = lax.axis_size("tensor")
    grid = Grid(shards)
    me = lax.axis_index("tensor")
    capacity = (9 * tok_count + 8 * experts - 1) // (8 * experts)
    share = 16 * -(-capacity // (16 * shards))
    padded = share * shards
    own_rows = experts * share
    tok_rows = tok_count // shards
    score_scale = head_size ** (-0.5)
    row_axis = ("y", "x")
    weight_axis = ("x", "y")
    win = [grid.gather_list(expert_in[0, k], weight_axis[k]) for k in range(2)]
    wout = [grid.gather_list(expert_out[0, k], weight_axis[k]) for k in range(2)]
    out_flat = out_weight.reshape(heads_here * head_size, model_width)
    out_all = lax.all_gather(out_flat, "tensor", axis=0, tiled=True)
    slot_token, token_slot = plan_slots(
        routes, fill_order, lengths, seq_len, experts, capacity, padded
    )
    own_slot = lax.dynamic_slice_in_dim(
        slot_token.reshape(experts, padded), me * share, share, 1
    ).reshape(own_rows)
    own_filled = (own_slot < tok_count)[:, None]
    own_index = jnp.minimum(own_slot, tok_count - 1)
    kept = (token_slot < experts * padded)[:, None]
    tok_expert = jnp.minimum(token_slot // padded, experts - 1)
    tok_rank = token_slot % padded
    tok_place = (tok_rank // share * experts + tok_expert) * share + tok_rank % share

    def to_experts(rows):
        picked = jnp.where(own_filled, rows[own_index], jnp.zeros((), rows.dtype))
        moved = lax.all_to_all(
            picked.reshape(experts, share, model_width),
            "dp",
            split_axis=0,
            concat_axis=0,
            tiled=True,
        )
        return moved.reshape(own_rows, model_width)

    def from_experts(rows):
        moved = lax.all_to_all(
            rows.reshape(experts, share, model_width), "dp", split_axis=0, concat_axis=0, tiled=True
        )
        every = gather_rows(grid, moved.reshape(own_rows, model_width))
        picked = every.reshape(shards * own_rows, model_width)[tok_place]
        return jnp.where(kept, picked, jnp.zeros((), rows.dtype)).astype(F32)

    grad_ret = to_experts(cotangent).astype(F32)
    input_rows = tokens.astype(F32)
    centre = input_rows - jnp.mean(input_rows, axis=1, keepdims=True)
    inverse_scale = lax.rsqrt(jnp.mean(centre * centre, axis=1, keepdims=True) + EPSILON)
    normed = centre * inverse_scale
    ln_in = (normed * norm_gain + norm_bias).astype(BF16)
    projected = jnp.einsum("td,dhe->the", ln_in, qkv_weight, preferred_element_type=F32).astype(
        BF16
    )
    projected = projected.reshape(seq_count, seq_len, heads_here, 3 * head_size)
    queries = projected[..., :head_size]
    key_vectors = projected[..., head_size : 2 * head_size]
    values = projected[..., 2 * head_size :]
    positions = jnp.arange(seq_len, dtype=jnp.int32)
    allowed = (positions[None, None, :] <= positions[None, :, None]) & (
        positions[None, None, :] < lengths[:, None, None]
    )

    def attention_probs(log_total):
        scores = (
            jnp.einsum("sqhd,skhd->shqk", queries, key_vectors, preferred_element_type=F32)
            * score_scale
        )
        scores = jnp.where(allowed[:, None], scores, -1e30)
        if log_total is None:
            row_max = jnp.max(scores, axis=-1, keepdims=True)
            log_total = row_max + jnp.log(
                jnp.sum(jnp.exp(scores - row_max), axis=-1, keepdims=True)
            )
        return (jnp.exp(scores - log_total), log_total)

    attention_weights, log_total = attention_probs(None)
    attended = jnp.einsum(
        "shqk,skhd->sqhd", attention_weights.astype(BF16), values, preferred_element_type=F32
    ).astype(BF16)
    attended = attended.reshape(tok_count, heads_here * head_size)
    every_attended = gather_rows(grid, attended)
    attended_all = jnp.swapaxes(every_attended, 0, 1).reshape(tok_count, -1)
    mixed = input_rows + dot(attended_all, out_all, ((1,), (0,)))
    sent = mixed.astype(BF16)
    expert_rows = to_experts(sent)
    centroid = centroids[0]
    gate = jax.nn.sigmoid(jnp.dot(expert_rows, centroid, preferred_element_type=F32))[:, None]
    current = expert_rows.astype(F32)
    saved = []
    for k in range(2):
        rows_in = jnp.concatenate(grid.gather_list(current.astype(BF16), row_axis[k]), axis=0)
        acts, slopes = ([], [])
        total = None
        for w_in, w_out in zip(win[k], wout[k]):
            act, slope = gelu_pair(dot(rows_in, w_in, ((1,), (0,))))
            term = dot(act, w_out, ((1,), (0,)))
            total = term if total is None else total + term
            acts.append(act)
            slopes.append(slope)
        parts = jnp.split(total, grid.parts[row_axis[k]], axis=0)
        current = current + grid.scatter_list(parts, row_axis[k])
        saved.append((rows_in, acts, slopes))
    output = (mixed + from_experts((gate * current).astype(BF16))).astype(BF16)
    grad_gate = jnp.sum(grad_ret * current, axis=1, keepdims=True)
    grad_logit = grad_gate * gate * (1.0 - gate)
    grad_current = gate * grad_ret
    grads_in = [None, None]
    grads_back = [None, None]
    for k in (1, 0):
        rows_in, acts, slopes = saved[k]
        branch = jnp.concatenate(grid.gather_list(grad_current.astype(BF16), row_axis[k]), axis=0)
        total = None
        in_parts, out_parts = ([], [])
        for w_in, w_out, act, slope in zip(win[k], wout[k], acts, slopes):
            grad_pre = (dot(branch, w_out, ((1,), (1,))) * slope.astype(F32)).astype(BF16)
            term = dot(grad_pre, w_in, ((1,), (1,)))
            total = term if total is None else total + term
            out_parts.append(dot(act, branch, ((0,), (0,))))
            in_parts.append(dot(rows_in, grad_pre, ((0,), (0,))))
        parts = jnp.split(total, grid.parts[row_axis[k]], axis=0)
        grad_current = grad_current + grid.scatter_list(parts, row_axis[k])
        grads_in[k] = grid.scatter_list(in_parts, weight_axis[k])
        grads_back[k] = grid.scatter_list(out_parts, weight_axis[k])
    grad_rows = (grad_current + grad_logit * centroid.astype(F32)[None, :]).astype(BF16)
    grad_centroid = lax.psum(
        jnp.sum(grad_logit * expert_rows.astype(F32), axis=0, keepdims=True), "tensor"
    )
    grad_mixed = cotangent.astype(F32) + from_experts(grad_rows)
    grad_attn = grad_mixed.astype(BF16)
    grad_out_local = dot(attended, grad_attn, ((0,), (0,))).reshape(
        heads_here, head_size, model_width
    )
    grad_attended = dot(grad_attn, out_flat, ((1,), (1,))).astype(BF16)
    grad_attended = grad_attended.reshape(seq_count, seq_len, heads_here, head_size)
    attention_weights, unused_total = attention_probs(log_total)
    grad_probs = jnp.einsum("sqhd,skhd->shqk", grad_attended, values, preferred_element_type=F32)
    row_delta = jnp.sum(attention_weights * grad_probs, axis=-1, keepdims=True)
    grad_scores = (attention_weights * (grad_probs - row_delta)).astype(BF16)
    grad_query = (
        jnp.einsum("shqk,skhd->sqhd", grad_scores, key_vectors, preferred_element_type=F32)
        * score_scale
    ).astype(BF16)
    grad_key = (
        jnp.einsum("shqk,sqhd->skhd", grad_scores, queries, preferred_element_type=F32)
        * score_scale
    ).astype(BF16)
    grad_value = jnp.einsum(
        "shqk,sqhd->skhd", attention_weights.astype(BF16), grad_attended, preferred_element_type=F32
    ).astype(BF16)
    grad_projected = jnp.concatenate([grad_query, grad_key, grad_value], axis=-1).reshape(
        tok_count, heads_here, 3 * head_size
    )
    grad_qkv_local = jnp.einsum("td,the->dhe", ln_in, grad_projected, preferred_element_type=F32)
    grad_ln_part = jnp.einsum("the,dhe->td", grad_projected, qkv_weight, preferred_element_type=F32)
    grad_ln = scatter_rows(grid, grad_ln_part.astype(BF16).reshape(shards, tok_rows, model_width))

    def own(rows):
        return lax.dynamic_slice_in_dim(rows, me * tok_rows, tok_rows, 0)

    own_scale = own(inverse_scale)
    own_normed = own(centre) * own_scale
    grad_normed = grad_ln * norm_gain
    mean_plain = jnp.mean(grad_normed, axis=1, keepdims=True)
    mean_cross = jnp.mean(grad_normed * own_normed, axis=1, keepdims=True)
    grad_input = own(grad_mixed) + own_scale * (grad_normed - mean_plain - own_normed * mean_cross)
    grad_tokens = gather_rows(grid, grad_input.astype(BF16)).reshape(tok_count, model_width)
    norm_parts = jnp.stack([jnp.sum(grad_ln * own_normed, axis=0), jnp.sum(grad_ln, axis=0)])
    norm_total = lax.dynamic_slice_in_dim(
        lax.psum(norm_parts, ("dp", "tensor")),
        me * (model_width // shards),
        model_width // shards,
        1,
    )
    grad_qkv_weight, grad_out_weight = lax.psum((grad_qkv_local, grad_out_local), "dp")
    return (
        output,
        grad_tokens,
        norm_total[0],
        norm_total[1],
        grad_qkv_weight,
        grad_out_weight,
        grad_centroid,
        jnp.stack(grads_in)[None],
        jnp.stack(grads_back)[None],
    )


def solution(mesh):
    return jax.shard_map(
        body,
        mesh=mesh,
        in_specs=(
            P("dp", None),
            P("dp"),
            P("dp", None),
            P("dp", None),
            P(),
            P(),
            P(None, "tensor", None),
            P("tensor", None, None),
            P("dp", None),
            P("dp", None, None, "tensor"),
            P("dp", None, "tensor", None),
            P("dp", None),
        ),
        out_specs=(
            P("dp", None),
            P("dp", None),
            P("tensor"),
            P("tensor"),
            P(None, "tensor", None),
            P("tensor", None, None),
            P("dp", None),
            P("dp", None, None, "tensor"),
            P("dp", None, "tensor", None),
        ),
        check_vma=False,
    )
```

profile of v0, /device:TPU:0, one launch (start us, length us, event | category | flops | bytes accessed | tf_op | source)
XLA Modules:
  0.0 1408.5 jit_solution(3828291646385503996)
XLA Ops:
  25.6 13.7 reshape.318
  46.0 19.2 %fusion = (f32[3,4,1024]{2,1,0:T(4,128)S(1)}, f32[3,4,1024,1024]{2,3,1,0:T(8,128)}) fusion(pred[3,1024,1024]{1,2,0:T(8,128)(4,1)S(1)} %broadcast_and_fusion, bf16[3,1024,4,64]{1,0,3,2:T(4,128)(2,1)S(1)} %get-tuple-element.29, bf16[3,1024,4,64]{1,0,3,2:T(4,128)(2,1)S(1)} %get-tuple-element.27), kind=kOutput, calls=%fused_computation.13 | convolution fusion | flops 1648349184 | bytes 56672256 | tf_op jit(solution)/shard_map/sqhd,skhd->shqk/dot_general | solution.py:218
  65.2 21.3 %exponential_reduce_fusion = f32[3,4,1024]{2,1,0:T(4,128)S(1)} fusion(f32[3,4,1024,1024]{2,3,1,0:T(8,128)} %get-tuple-element.54, f32[3,4,1024]{2,1,0:T(4,128)S(1)} %get-tuple-element.53, pred[3,1024,1024]{1,2,0:T(8,128)(4,1)S(1)} %broadcast_and_fusion), kind=kLoop, calls=%fused_computation.11 | loop fusion | flops 50319360 | bytes 53575680 | tf_op jit(solution)/shard_map/reduce_sum | solution.py:225
  86.6 20.1 %fusion.39 = bf16[3,1024,4,64]{1,3,2,0:T(8,128)(2,1)S(1)} fusion(bf16[3,1024,4,64]{1,0,3,2:T(4,128)(2,1)S(1)} %get-tuple-element.28, f32[3,4,1024,1024]{2,3,1,0:T(8,128)} %get-tuple-element.54, f32[3,4,1024]{2,1,0:T(4,128)S(1)} %log_add_fusion, pred[3,1024,1024]{1,2,0:T(8,128)(4,1)S(1)} %broadcast_and_fusion), kind=kOutput, calls=%fused_computation.133 | convolution fusion | flops 1661730816 | bytes 56672256 | tf_op jit(solution)/shard_map/shqk,skhd->sqhd/dot_general | solution.py:230
  120.9 19.4 %gather_fusion = pred[3072]{0:T(1024)(128)(4,1)S(1)} fusion(pred[3072]{0:T(1024)(128)(4,1)S(1)} %fusion.60, s32[3072]{0:T(1024)S(1)} %broadcast_clamp_fusion), kind=kCustom, calls=%fused_computation | custom fusion | bytes 18432 | tf_op jit(solution)/shard_map/gather | solution.py:109
  140.3 17.4 %gather_fusion.1 = s32[3072]{0:T(1024)S(1)} fusion(s32[3072]{0:T(1024)S(1)} %bitcast.249, s32[3072]{0:T(1024)S(1)} %broadcast_clamp_fusion), kind=kCustom, calls=%fused_computation.1 | custom fusion | bytes 36864 | tf_op jit(solution)/shard_map/gather | solution.py:108
  207.4 14.0 fusion.2
  245.4 37.3 %all-to-all-done = bf16[8,112,1024]{2,1,0:T(8,128)(2,1)S(1)} async-done(((bf16[8,112,1024]{2,1,0:T(8,128)(2,1)}), bf16[8,112,1024]{2,1,0:T(8,128)(2,1)S(1)}, u32[]{:S(2)}, u32[]{:S(2)}) %all-to-all-start) | async-done | bytes 1835040 | tf_op jit(solution)/shard_map/all_to_all | solution.py:181
  292.6 31.6 %collective-permute-done.6 = bf16[896,1024]{1,0:T(8,128)(2,1)S(1)} collective-permute-done((bf16[896,1024]{1,0:T(8,128)(2,1)S(1)}, bf16[896,1024]{1,0:T(8,128)(2,1)S(1)}, u32[]{:S(2)}, u32[]{:S(2)}) %collective-permute-start.6) | collective-permute-done | bytes 1835040 | tf_op jit(solution)/shard_map/ppermute | solution.py:35
  362.3 36.4 %collective-permute-done.9 = bf16[896,1024]{1,0:T(8,128)(2,1)} collective-permute-done((bf16[896,1024]{1,0:T(8,128)(2,1)}, bf16[896,1024]{1,0:T(8,128)(2,1)}, u32[]{:S(2)}, u32[]{:S(2)}) %collective-permute-start.9) | collective-permute-done | bytes 1835040 | tf_op jit(solution)/shard_map/ppermute | solution.py:35
  409.3 34.3 %collective-permute-done.11 = bf16[1024,1024]{1,0:T(8,128)(2,1)} collective-permute-done((bf16[1024,1024]{1,0:T(8,128)(2,1)}, bf16[1024,1024]{1,0:T(8,128)(2,1)}, u32[]{:S(2)}, u32[]{:S(2)}) %collective-permute-start.11) | collective-permute-done | bytes 2097184 | tf_op jit(solution)/shard_map/ppermute | solution.py:35
  465.0 15.5 %collective-permute-done.20 = bf16[896,1024]{1,0:T(8,128)(2,1)S(1)} collective-permute-done((bf16[896,1024]{1,0:T(8,128)(2,1)S(1)}, bf16[896,1024]{1,0:T(8,128)(2,1)S(1)}, u32[]{:S(2)}, u32[]{:S(2)}) %collective-permute-start.20) | collective-permute-done | bytes 1835040 | tf_op jit(solution)/shard_map/ppermute | solution.py:35
  540.4 19.4 %collective-permute-done.21 = bf16[896,1024]{1,0:T(8,128)(2,1)S(1)} collective-permute-done((bf16[896,1024]{1,0:T(8,128)(2,1)S(1)}, bf16[896,1024]{1,0:T(8,128)(2,1)S(1)}, u32[]{:S(2)}, u32[]{:S(2)}) %collective-permute-start.21) | collective-permute-done | bytes 1835040 | tf_op jit(solution)/shard_map/ppermute | solution.py:35
  559.8 33.0 %collective-permute-done.13 = bf16[896,1024]{1,0:T(8,128)(2,1)} collective-permute-done((bf16[896,1024]{1,0:T(8,128)(2,1)S(1)}, bf16[896,1024]{1,0:T(8,128)(2,1)}, u32[]{:S(2)}, u32[]{:S(2)}) %collective-permute-start.13) | collective-permute-done | bytes 1835040 | tf_op jit(solution)/shard_map/ppermute | solution.py:35
  600.3 34.3 %collective-permute-done.22 = bf16[896,1024]{1,0:T(8,128)(2,1)S(1)} collective-permute-done((bf16[896,1024]{1,0:T(8,128)(2,1)S(1)}, bf16[896,1024]{1,0:T(8,128)(2,1)S(1)}, u32[]{:S(2)}, u32[]{:S(2)}) %collective-permute-start.22) | collective-permute-done | bytes 1835040 | tf_op jit(solution)/shard_map/ppermute | solution.py:35
  672.0 33.6 %collective-permute-done.23 = bf16[896,1024]{1,0:T(8,128)(2,1)} collective-permute-done((bf16[896,1024]{1,0:T(8,128)(2,1)}, bf16[896,1024]{1,0:T(8,128)(2,1)}, u32[]{:S(2)}, u32[]{:S(2)}) %collective-permute-start.23) | collective-permute-done | bytes 1835040 | tf_op jit(solution)/shard_map/ppermute | solution.py:35
  788.7 34.7 %collective-permute-done.43 = bf16[1024,1024]{1,0:T(8,128)(2,1)} collective-permute-done((bf16[1024,1024]{1,0:T(8,128)(2,1)}, bf16[1024,1024]{1,0:T(8,128)(2,1)}, u32[]{:S(2)}, u32[]{:S(2)}) %collective-permute-start.43) | collective-permute-done | bytes 2097184 | tf_op jit(solution)/shard_map/ppermute | solution.py:35
  869.3 13.7 collective-permute-done.15
  904.9 17.3 %collective-permute-done.25 = bf16[448,1024]{1,0:T(8,128)(2,1)S(1)} collective-permute-done((bf16[448,1024]{1,0:T(8,128)(2,1)S(1)}, bf16[448,1024]{1,0:T(8,128)(2,1)S(1)}, u32[]{:S(2)}, u32[]{:S(2)}) %collective-permute-start.25) | collective-permute-done | bytes 917536 | tf_op jit(solution)/shard_map/ppermute | solution.py:35
  933.0 16.1 %collective-permute-done.18 = bf16[448,1024]{1,0:T(8,128)(2,1)S(1)} collective-permute-done((bf16[448,1024]{1,0:T(8,128)(2,1)}, bf16[448,1024]{1,0:T(8,128)(2,1)S(1)}, u32[]{:S(2)}, u32[]{:S(2)}) %collective-permute-start.18) | collective-permute-done | bytes 917536 | tf_op jit(solution)/shard_map/ppermute | solution.py:35
  951.7 15.2 %collective-permute-done.28 = bf16[448,1024]{1,0:T(8,128)(2,1)S(1)} collective-permute-done((bf16[448,1024]{1,0:T(8,128)(2,1)S(1)}, bf16[448,1024]{1,0:T(8,128)(2,1)S(1)}, u32[]{:S(2)}, u32[]{:S(2)}) %collective-permute-start.28) | collective-permute-done | bytes 917536 | tf_op jit(solution)/shard_map/ppermute | solution.py:35
  967.9 18.9 %collective-permute-done.19 = bf16[448,1024]{1,0:T(8,128)(2,1)S(1)} collective-permute-done((bf16[448,1024]{1,0:T(8,128)(2,1)S(1)}, bf16[448,1024]{1,0:T(8,128)(2,1)S(1)}, u32[]{:S(2)}, u32[]{:S(2)}) %collective-permute-start.19) | collective-permute-done | bytes 917536 | tf_op jit(solution)/shard_map/ppermute | solution.py:35
  986.8 19.7 %collective-permute-done.29 = bf16[448,1024]{1,0:T(8,128)(2,1)S(1)} collective-permute-done((bf16[448,1024]{1,0:T(8,128)(2,1)S(1)}, bf16[448,1024]{1,0:T(8,128)(2,1)S(1)}, u32[]{:S(2)}, u32[]{:S(2)}) %collective-permute-start.29) | collective-permute-done | bytes 917536 | tf_op jit(solution)/shard_map/ppermute | solution.py:35
  1007.8 19.9 %gather_fusion.3 = bf16[3072,1024]{1,0:T(8,128)(2,1)} fusion(bf16[3584,1024]{1,0:T(8,128)(2,1)} %bitcast.37, s32[3072]{0:T(1024)S(1)} %fusion.66), kind=kCustom, calls=%fused_computation.3 | custom fusion | bytes 12595200 | tf_op jit(solution)/shard_map/gather | solution.py:195
  1027.7 19.9 %gather_fusion.5 = bf16[3072,1024]{1,0:T(8,128)(2,1)} fusion(bf16[3584,1024]{1,0:T(8,128)(2,1)} %bitcast.51, s32[3072]{0:T(1024)S(1)} %fusion.66), kind=kCustom, calls=%fused_computation.5 | custom fusion | bytes 12595200 | tf_op jit(solution)/shard_map/gather | solution.py:195
  1047.6 17.5 %convert_add_fusion.1 = (f32[3072,1024]{1,0:T(8,128)S(1)}, bf16[3072,1024]{1,0:T(8,128)(2,1)}) fusion(bf16[3072,1024]{1,0:T(8,128)(2,1)} %param.23, bf16[3072,1024]{1,0:T(8,128)(2,1)} %gather_fusion.5, pred[3072]{0:T(1024)(128)(4,1)S(1)} %broadcast_compare_fusion, bf16[3072,1024]{1,0:T(8,128)(2,1)} %gather_fusion.3, f32[3072,1024]{1,0:T(8,128)} %get-tuple-element.56, ...), kind=kLoop, calls=%fused_computation.19 | loop fusion | flops 31457280 | bytes 56626176 | tf_op jit(solution)/shard_map/add | solution.py:281
  1078.7 36.9 %multiply_reduce_fusion = (f32[3,4,1024]{2,1,0:T(4,128)S(1)}, f32[3,4,1024,1024]{2,3,1,0:T(8,128)}) fusion(f32[3,4,1024,1024]{2,3,1,0:T(8,128)} %get-tuple-element.54, f32[3,4,1024]{2,1,0:T(4,128)S(1)} %copy-done.33, pred[3,1024,1024]{1,2,0:T(8,128)(4,1)} %copy-done.3, bf16[3,1024,4,64]{1,3,2,0:T(8,128)(2,1)S(1)} %copy.37, ...), kind=kOutput, calls=%fused_computation.9 | convolution fusion | flops 1673515008 | bytes 107053056 | tf_op jit(solution)/shard_map/sqhd,skhd->shqk/dot_general | solution.py:289
  1115.6 42.3 %multiply_convert_fusion = bf16[3,4,1024,1024]{2,3,1,0:T(8,128)(2,1)} fusion(f32[3,4,1024,1024]{2,3,1,0:T(8,128)} %get-tuple-element.66, f32[3,4,1024,1024]{2,3,1,0:T(8,128)} %get-tuple-element.54, f32[3,4,1024]{2,1,0:T(4,128)S(1)} %get-tuple-element.65, f32[3,4,1024]{2,1,0:T(4,128)S(1)} %copy-done.33, pred[3,1024,1024]{1,2,0:T(8,128)(4,1)} %copy-done.3), kind=kLoop, calls=%fused_computation.8 | loop fusion | flops 75497472 | bytes 129073152 | tf_op jit(solution)/shard_map/convert_element_type | solution.py:291
  1171.3 14.0 fusion.42
  1185.4 20.3 %fusion.40 = bf16[3,1024,4,64]{1,3,2,0:T(8,128)(2,1)S(1)} fusion(bf16[3,1024,4,64]{1,3,2,0:T(8,128)(2,1)} %copy-done.12, f32[3,4,1024,1024]{2,3,1,0:T(8,128)} %get-tuple-element.54, f32[3,4,1024]{2,1,0:T(4,128)S(1)} %copy-done.33, pred[3,1024,1024]{1,2,0:T(8,128)(4,1)} %copy-done.3), kind=kOutput, calls=%fused_computation.134 | convolution fusion | flops 1661730816 | bytes 56672256 | tf_op jit(solution)/shard_map/shqk,sqhd->skhd/dot_general | solution.py:300
  1308.7 49.7 %psum.28 = f32[2,1024]{1,0:T(2,128)S(1)} all-reduce(f32[2,1024]{1,0:T(2,128)S(1)} %pad_maximum_fusion.6), channel_id=1, replica_groups=mesh['dp'=8,'tensor'=4] {'dp','tensor'}, use_global_device_ids=true, to_apply=%region_15.16 | all-reduce | flops 2048 | bytes 16384 | tf_op jit(solution)/shard_map/psum | solution.py:322
  1379.8 16.4 %all-reduce.3.cloned.1.call-done = (f32[1024,4,192]{0,2,1:T(8,128)}, f32[4,64,1024]{2,1,0:T(8,128)}) async-done(((f32[1024,4,192]{0,2,1:T(8,128)}, f32[4,64,1024]{2,1,0:T(8,128)}), (f32[1024,4,192]{0,2,1:T(8,128)}, f32[4,64,1024]{2,1,0:T(8,128)})) %all-reduce.3.cloned.1.call-update) | async-done | bytes 4194320 | tf_op jit(solution)/shard_map/psum | solution.py:327
  (388 shorter events, 619.9 us)
Async XLA Ops:
  7.2 200.2 %all-gather.2.cloned.1.call-start = ((), (), s32[]{:S(2)}) async-start(), calls=%async_computation.4 | async-start | bytes 2621440 | tf_op jit(solution)/shard_map/all_gather | solution.py:165
  110.7 75.7 %collective-permute-start = (bf16[1536,256]{0,1:T(8,128)(2,1)}, bf16[1536,256]{0,1:T(8,128)(2,1)}, u32[]{:S(2)}, u32[]{:S(2)}) collective-permute-start(bf16[1536,256]{0,1:T(8,128)(2,1)} %get-tuple-element.44), channel_id=1, source_target_pairs={{1,0},{0,1},{3,2},{2,3},{5,4},{4,5},{7,6},{6,7},{9,8},{8,9},{11,10... | collective-permute-start | bytes 2359304 | tf_op jit(solution)/shard_map/ppermute | solution.py:35
  113.6 80.4 %collective-permute-start.2 = (bf16[1536,256]{0,1:T(8,128)(2,1)}, bf16[1536,256]{0,1:T(8,128)(2,1)}, u32[]{:S(2)}, u32[]{:S(2)}) collective-permute-start(bf16[1536,256]{0,1:T(8,128)(2,1)} %get-tuple-element.44), channel_id=1, source_target_pairs={{2,0},{3,1},{0,2},{1,3},{6,4},{7,5},{4,6},{5,7},{10,8},{11,9},{8,1... | collective-permute-start | bytes 2359304 | tf_op jit(solution)/shard_map/ppermute | solution.py:35
  115.1 76.8 %collective-permute-start.1 = (bf16[1536,256]{0,1:T(8,128)(2,1)}, bf16[1536,256]{0,1:T(8,128)(2,1)}, u32[]{:S(2)}, u32[]{:S(2)}) collective-permute-start(bf16[1536,256]{0,1:T(8,128)(2,1)} %get-tuple-element.43), channel_id=1, source_target_pairs={{1,0},{0,1},{3,2},{2,3},{5,4},{4,5},{7,6},{6,7},{9,8},{8,9},{11,10... | collective-permute-start | bytes 2359304 | tf_op jit(solution)/shard_map/ppermute | solution.py:35
  115.7 72.7 %collective-permute-start.3 = (bf16[1536,256]{0,1:T(8,128)(2,1)}, bf16[1536,256]{0,1:T(8,128)(2,1)}, u32[]{:S(2)}, u32[]{:S(2)}) collective-permute-start(bf16[1536,256]{0,1:T(8,128)(2,1)} %get-tuple-element.43), channel_id=1, source_target_pairs={{2,0},{3,1},{0,2},{1,3},{6,4},{7,5},{4,6},{5,7},{10,8},{11,9},{8,1... | collective-permute-start | bytes 2359304 | tf_op jit(solution)/shard_map/ppermute | solution.py:35
  234.3 48.3 %all-to-all-start = ((bf16[8,112,1024]{2,1,0:T(8,128)(2,1)}), bf16[8,112,1024]{2,1,0:T(8,128)(2,1)S(1)}, u32[]{:S(2)}, u32[]{:S(2)}) async-start(bf16[8,112,1024]{2,1,0:T(8,128)(2,1)} %get-tuple-element.51), calls=%async_computation | async-start | bytes 3670016 | tf_op jit(solution)/shard_map/all_to_all | solution.py:181
  243.9 48.7 %collective-permute-start.7 = (bf16[1024,1024]{1,0:T(8,128)(2,1)}, bf16[1024,1024]{1,0:T(8,128)(2,1)}, u32[]{:S(2)}, u32[]{:S(2)}) collective-permute-start(bf16[1024,1024]{1,0:T(8,128)(2,1)} %get-tuple-element.35), channel_id=1, source_target_pairs={{1,0},{0,1},{3,2},{2,3},{5,4},{4,5},{7,6},{6,7},{9,8},{8,9},{11,10... | collective-permute-start | bytes 6291464 | tf_op jit(solution)/shard_map/ppermute | solution.py:35
  287.9 58.7 %collective-permute-start.8 = (bf16[1024,1024]{1,0:T(8,128)(2,1)S(1)}, bf16[1024,1024]{1,0:T(8,128)(2,1)S(1)}, u32[]{:S(2)}, u32[]{:S(2)}) collective-permute-start(bf16[1024,1024]{1,0:T(8,128)(2,1)S(1)} %get-tuple-element.33), channel_id=1, source_target_pairs={{1,0},{0,1},{3,2},{2,3},{5,4},{4,5},{7,6},{6,7},{9,8},{8,9},{11,10... | collective-permute-start | bytes 6291464 | tf_op jit(solution)/shard_map/ppermute | solution.py:35
  355.4 43.3 %collective-permute-start.9 = (bf16[896,1024]{1,0:T(8,128)(2,1)}, bf16[896,1024]{1,0:T(8,128)(2,1)}, u32[]{:S(2)}, u32[]{:S(2)}) collective-permute-start(bf16[896,1024]{1,0:T(8,128)(2,1)} %split.75), channel_id=1, source_target_pairs={{2,0},{3,1},{0,2},{1,3},{6,4},{7,5},{4,6},{5,7},{10,8},{11,9},{8,1... | collective-permute-start | bytes 5505032 | tf_op jit(solution)/shard_map/ppermute | solution.py:35
  356.6 49.0 %all-to-all-start.2 = ((bf16[8,112,1024]{2,1,0:T(8,128)(2,1)}), bf16[8,112,1024]{2,1,0:T(8,128)(2,1)}, u32[]{:S(2)}, u32[]{:S(2)}) async-start(bf16[8,112,1024]{2,1,0:T(8,128)(2,1)} %get-tuple-element.52), calls=%async_computation.2 | async-start | bytes 3670016 | tf_op jit(solution)/shard_map/all_to_all | solution.py:181
  361.4 82.3 %collective-permute-start.11 = (bf16[1024,1024]{1,0:T(8,128)(2,1)}, bf16[1024,1024]{1,0:T(8,128)(2,1)}, u32[]{:S(2)}, u32[]{:S(2)}) collective-permute-start(bf16[1024,1024]{1,0:T(8,128)(2,1)} %get-tuple-element.34), channel_id=1, source_target_pairs={{2,0},{3,1},{0,2},{1,3},{6,4},{7,5},{4,6},{5,7},{10,8},{11,9},{8,1... | collective-permute-start | bytes 6291464 | tf_op jit(solution)/shard_map/ppermute | solution.py:35
  403.5 43.3 %collective-permute-start.10 = (bf16[896,1024]{1,0:T(8,128)(2,1)}, bf16[896,1024]{1,0:T(8,128)(2,1)}, u32[]{:S(2)}, u32[]{:S(2)}) collective-permute-start(bf16[896,1024]{1,0:T(8,128)(2,1)} %fusion.43), channel_id=1, source_target_pairs={{1,0},{0,1},{3,2},{2,3},{5,4},{4,5},{7,6},{6,7},{9,8},{8,9},{11,10... | collective-permute-start | bytes 5505032 | tf_op jit(solution)/shard_map/ppermute | solution.py:35
  407.5 73.0 %collective-permute-start.20 = (bf16[896,1024]{1,0:T(8,128)(2,1)S(1)}, bf16[896,1024]{1,0:T(8,128)(2,1)S(1)}, u32[]{:S(2)}, u32[]{:S(2)}) collective-permute-start(bf16[896,1024]{1,0:T(8,128)(2,1)S(1)} %fusion.26), channel_id=1, source_target_pairs={{1,0},{0,1},{3,2},{2,3},{5,4},{4,5},{7,6},{6,7},{9,8},{8,9},{11,10... | collective-permute-start | bytes 5505032 | tf_op jit(solution)/shard_map/ppermute | solution.py:35
  408.2 88.7 %collective-permute-start.12 = (bf16[1024,1024]{1,0:T(8,128)(2,1)}, bf16[1024,1024]{1,0:T(8,128)(2,1)S(1)}, u32[]{:S(2)}, u32[]{:S(2)}) collective-permute-start(bf16[1024,1024]{1,0:T(8,128)(2,1)} %get-tuple-element.32), channel_id=1, source_target_pairs={{2,0},{3,1},{0,2},{1,3},{6,4},{7,5},{4,6},{5,7},{10,8},{11,9},{8,1... | collective-permute-start | bytes 6291464 | tf_op jit(solution)/shard_map/ppermute | solution.py:35
  538.8 54.1 %collective-permute-start.13 = (bf16[896,1024]{1,0:T(8,128)(2,1)S(1)}, bf16[896,1024]{1,0:T(8,128)(2,1)}, u32[]{:S(2)}, u32[]{:S(2)}) collective-permute-start(bf16[896,1024]{1,0:T(8,128)(2,1)S(1)} %split.74), channel_id=1, source_target_pairs={{1,0},{0,1},{3,2},{2,3},{5,4},{4,5},{7,6},{6,7},{9,8},{8,9},{11,10... | collective-permute-start | bytes 5505032 | tf_op jit(solution)/shard_map/ppermute | solution.py:35
  713.9 50.9 %all-to-all-start.1 = ((bf16[8,112,1024]{2,1,0:T(8,128)(2,1)}), bf16[8,112,1024]{2,1,0:T(8,128)(2,1)}, u32[]{:S(2)}, u32[]{:S(2)}) async-start(bf16[8,112,1024]{2,1,0:T(8,128)(2,1)} %bitcast.268), calls=%async_computation.1 | async-start | bytes 3670016 | tf_op jit(solution)/shard_map/all_to_all | solution.py:191
  730.0 48.9 %collective-permute-start.45 = (bf16[1024,1024]{1,0:T(8,128)(2,1)}, bf16[1024,1024]{1,0:T(8,128)(2,1)}, u32[]{:S(2)}, u32[]{:S(2)}) collective-permute-start(bf16[1024,1024]{1,0:T(8,128)(2,1)} %convolution_convert_fusion.1), channel_id=1, source_target_pairs={{2,0},{3,1},{0,2},{1,3},{6,4},{7,5},{4,6},{5,7},{10,8},{11,9},{8,1... | collective-permute-start | bytes 6291464 | tf_op jit(solution)/shard_map/ppermute | solution.py:35
  738.6 84.8 %collective-permute-start.43 = (bf16[1024,1024]{1,0:T(8,128)(2,1)}, bf16[1024,1024]{1,0:T(8,128)(2,1)}, u32[]{:S(2)}, u32[]{:S(2)}) collective-permute-start(bf16[1024,1024]{1,0:T(8,128)(2,1)} %convolution_convert_fusion.3), channel_id=1, source_target_pairs={{2,0},{3,1},{0,2},{1,3},{6,4},{7,5},{4,6},{5,7},{10,8},{11,9},{8,1... | collective-permute-start | bytes 6291464 | tf_op jit(solution)/shard_map/ppermute | solution.py:35
  764.8 84.2 %all-to-all-start.3 = ((bf16[8,112,1024]{2,1,0:T(8,128)(2,1)}), bf16[8,112,1024]{2,1,0:T(8,128)(2,1)}, u32[]{:S(2)}, u32[]{:S(2)}) async-start(bf16[8,112,1024]{2,1,0:T(8,128)(2,1)} %bitcast.267), calls=%async_computation.3 | async-start | bytes 3670016 | tf_op jit(solution)/shard_map/all_to_all | solution.py:191
  769.1 627.1 %all-reduce.3.cloned.1.call-start = ((), (), s32[]{:S(2)}) async-start(), calls=%async_computation.5 | async-start | bytes 8388608 | tf_op jit(solution)/shard_map/psum | solution.py:327
  850.6 51.9 %collective-permute-start.24 = (bf16[448,1024]{1,0:T(8,128)(2,1)S(1)}, bf16[448,1024]{1,0:T(8,128)(2,1)S(1)}, u32[]{:S(2)}, u32[]{:S(2)}) collective-permute-start(bf16[448,1024]{1,0:T(8,128)(2,1)S(1)} %bitcast.283), channel_id=1, source_target_pairs={{1,0},{0,1},{3,2},{2,3},{5,4},{4,5},{7,6},{6,7},{9,8},{8,9},{11,10... | collective-permute-start | bytes 2752520 | tf_op jit(solution)/shard_map/ppermute | solution.py:35
  866.0 58.5 %collective-permute-start.26 = (bf16[448,1024]{1,0:T(8,128)(2,1)S(1)}, bf16[448,1024]{1,0:T(8,128)(2,1)S(1)}, u32[]{:S(2)}, u32[]{:S(2)}) collective-permute-start(bf16[448,1024]{1,0:T(8,128)(2,1)S(1)} %bitcast.284), channel_id=1, source_target_pairs={{2,0},{3,1},{0,2},{1,3},{6,4},{7,5},{4,6},{5,7},{10,8},{11,9},{8,1... | collective-permute-start | bytes 2752520 | tf_op jit(solution)/shard_map/ppermute | solution.py:35
  890.2 327.1 %collective-permute-start.44 = (bf16[1024,1024]{1,0:T(8,128)(2,1)}, bf16[1024,1024]{1,0:T(8,128)(2,1)}, u32[]{:S(2)}, u32[]{:S(2)}) collective-permute-start(bf16[1024,1024]{1,0:T(8,128)(2,1)} %convolution_convert_fusion.2), channel_id=1, source_target_pairs={{1,0},{0,1},{3,2},{2,3},{5,4},{4,5},{7,6},{6,7},{9,8},{8,9},{11,10... | collective-permute-start | bytes 6291464 | tf_op jit(solution)/shard_map/ppermute | solution.py:35
  902.5 46.6 %collective-permute-start.18 = (bf16[448,1024]{1,0:T(8,128)(2,1)}, bf16[448,1024]{1,0:T(8,128)(2,1)S(1)}, u32[]{:S(2)}, u32[]{:S(2)}) collective-permute-start(bf16[448,1024]{1,0:T(8,128)(2,1)} %collective-permute-done.14), channel_id=1, source_target_pairs={{2,0},{3,1},{0,2},{1,3},{6,4},{7,5},{4,6},{5,7},{10,8},{11,9},{8,1... | collective-permute-start | bytes 2752520 | tf_op jit(solution)/shard_map/ppermute | solution.py:35
  922.2 44.8 %collective-permute-start.28 = (bf16[448,1024]{1,0:T(8,128)(2,1)S(1)}, bf16[448,1024]{1,0:T(8,128)(2,1)S(1)}, u32[]{:S(2)}, u32[]{:S(2)}) collective-permute-start(bf16[448,1024]{1,0:T(8,128)(2,1)S(1)} %collective-permute-done.24), channel_id=1, source_target_pairs={{2,0},{3,1},{0,2},{1,3},{6,4},{7,5},{4,6},{5,7},{10,8},{11,9},{8,1... | collective-permute-start | bytes 2752520 | tf_op jit(solution)/shard_map/ppermute | solution.py:35
  924.5 62.2 %collective-permute-start.19 = (bf16[448,1024]{1,0:T(8,128)(2,1)S(1)}, bf16[448,1024]{1,0:T(8,128)(2,1)S(1)}, u32[]{:S(2)}, u32[]{:S(2)}) collective-permute-start(bf16[448,1024]{1,0:T(8,128)(2,1)S(1)} %collective-permute-done.17), channel_id=1, source_target_pairs={{1,0},{0,1},{3,2},{2,3},{5,4},{4,5},{7,6},{6,7},{9,8},{8,9},{11,10... | collective-permute-start | bytes 2752520 | tf_op jit(solution)/shard_map/ppermute | solution.py:35
  929.5 77.0 %collective-permute-start.29 = (bf16[448,1024]{1,0:T(8,128)(2,1)S(1)}, bf16[448,1024]{1,0:T(8,128)(2,1)S(1)}, u32[]{:S(2)}, u32[]{:S(2)}) collective-permute-start(bf16[448,1024]{1,0:T(8,128)(2,1)S(1)} %collective-permute-done.27), channel_id=1, source_target_pairs={{1,0},{0,1},{3,2},{2,3},{5,4},{4,5},{7,6},{6,7},{9,8},{8,9},{11,10... | collective-permute-start | bytes 2752520 | tf_op jit(solution)/shard_map/ppermute | solution.py:35
  949.2 288.1 %collective-permute-start.42 = (bf16[1024,1024]{1,0:T(8,128)(2,1)}, bf16[1024,1024]{1,0:T(8,128)(2,1)}, u32[]{:S(2)}, u32[]{:S(2)}) collective-permute-start(bf16[1024,1024]{1,0:T(8,128)(2,1)} %convolution_convert_fusion.4), channel_id=1, source_target_pairs={{1,0},{0,1},{3,2},{2,3},{5,4},{4,5},{7,6},{6,7},{9,8},{8,9},{11,10... | collective-permute-start | bytes 6291464 | tf_op jit(solution)/shard_map/ppermute | solution.py:35
  1293.1 65.9 %collective-permute-start.36 = (bf16[384,1024]{1,0:T(8,128)(2,1)}, bf16[384,1024]{1,0:T(8,128)(2,1)S(1)}, u32[]{:S(2)}, u32[]{:S(2)}) collective-permute-start(bf16[384,1024]{1,0:T(8,128)(2,1)} %get-tuple-element.42), channel_id=1, source_target_pairs={{1,0},{0,1},{3,2},{2,3},{5,4},{4,5},{7,6},{6,7},{9,8},{8,9},{11,10... | collective-permute-start | bytes 2359304 | tf_op jit(solution)/shard_map/ppermute | solution.py:35
  1293.6 67.7 %collective-permute-start.39 = (bf16[384,1024]{1,0:T(8,128)(2,1)}, bf16[384,1024]{1,0:T(8,128)(2,1)S(1)}, u32[]{:S(2)}, u32[]{:S(2)}) collective-permute-start(bf16[384,1024]{1,0:T(8,128)(2,1)} %get-tuple-element.41), channel_id=1, source_target_pairs={{2,0},{3,1},{0,2},{1,3},{6,4},{7,5},{4,6},{5,7},{10,8},{11,9},{8,1... | collective-permute-start | bytes 2359304 | tf_op jit(solution)/shard_map/ppermute | solution.py:35
  1297.9 65.0 %collective-permute-start.37 = (bf16[384,1024]{1,0:T(8,128)(2,1)}, bf16[384,1024]{1,0:T(8,128)(2,1)}, u32[]{:S(2)}, u32[]{:S(2)}) collective-permute-start(bf16[384,1024]{1,0:T(8,128)(2,1)} %get-tuple-element.41), channel_id=1, source_target_pairs={{1,0},{0,1},{3,2},{2,3},{5,4},{4,5},{7,6},{6,7},{9,8},{8,9},{11,10... | collective-permute-start | bytes 2359304 | tf_op jit(solution)/shard_map/ppermute | solution.py:35
  1299.3 65.7 %collective-permute-start.38 = (bf16[384,1024]{1,0:T(8,128)(2,1)}, bf16[384,1024]{1,0:T(8,128)(2,1)}, u32[]{:S(2)}, u32[]{:S(2)}) collective-permute-start(bf16[384,1024]{1,0:T(8,128)(2,1)} %get-tuple-element.42), channel_id=1, source_target_pairs={{2,0},{3,1},{0,2},{1,3},{6,4},{7,5},{4,6},{5,7},{10,8},{11,9},{8,1... | collective-permute-start | bytes 2359304 | tf_op jit(solution)/shard_map/ppermute | solution.py:35
  (97 other events, 2634.6 us)
Sparse Core Ops, SparseCore 0:
  115.9 50.9 all-gather.1
  1298.0 98.1 all-reduce.2
where the time goes:
time: 1420 us; the launch traced here: 1410 us
  waiting for transfers between devices  494 us (35%)
  matrix products  350 us (25%)
  local copies, waits for them, and re-layouts  259 us (18%)
  other arithmetic  150 us (11%)
  starting transfers between devices  79.7 us (6%)
  blocking collectives  60.2 us (4%)
  between operations  15.8 us (1%)
    ppermute x46, waiting for transfers between devices, fetch(): return lax.ppermute(value, 'tensor', self._pairs(axis, shift))  439 us
    dot_general x27, matrix products, dot(): lax.dot_general(a, b, (contract, ((), ())), preferred_element_type=F32)  207 us
    ppermute x46, starting transfers between devices, fetch(): return lax.ppermute(value, 'tensor', self._pairs(axis, shift))  58.3 us
    psum x1, blocking collectives, body(): lax.psum(norm_parts, ('dp', 'tensor'))  49.7 us
    convert_element_type x1, other arithmetic, body(): grad_scores = (attention_weights * (grad_probs - row_delta)).astype(BF16)  42.3 us
    gather x2, local copies, waits for them, and re-layouts, from_experts(): picked = every.reshape(shards * own_rows, model_width)[tok_place]  39.8 us
    all_to_all x2, waiting for transfers between devices, to_experts(): lax.all_to_all(picked.reshape(experts, share, model_width), 'dp', split_a...  37.3 us
    dot_general x1, matrix products, body(): jnp.einsum('sqhd,skhd->shqk', grad_attended, values, preferred_element_ty...  36.9 us
  transfers between devices with their start and end apart: 52, of which 31 were waited for; matrix products, arithmetic and copies ran while one was open for 37% of the time, Pallas kernels for 0%

commit v1 on v0

--- a/solution.py
+++ b/solution.py
@@ -178,13 +178,19 @@
 
     def to_experts(rows):
         picked = jnp.where(own_filled, rows[own_index], jnp.zeros((), rows.dtype))
-        moved = lax.all_to_all(
-            picked.reshape(experts, share, model_width),
-            "dp",
-            split_axis=0,
-            concat_axis=0,
-            tiled=True,
-        )
+        shard = picked.reshape(experts, share, model_width)
+        ways, here = (lax.axis_size("dp"), lax.axis_index("dp"))
+        width_2 = shard.shape[0] // ways
+        dims = list(shard.shape)
+        dims[0] = width_2
+        height = dims[0]
+        dims[0] = height * ways
+        moved = jnp.zeros(dims, shard.dtype)
+        for mask in range(ways):
+            part = lax.dynamic_slice_in_dim(shard, (here ^ mask) * width_2, width_2, axis=0)
+            if mask:
+                part = lax.ppermute(part, "dp", [(d, d ^ mask) for d in range(ways)])
+            moved = lax.dynamic_update_slice_in_dim(moved, part, (here ^ mask) * height, axis=0)
         return moved.reshape(own_rows, model_width)
 
     def from_experts(rows):

time: 1420 us -> 1440 us (1.014)
  starting transfers between devices: 79.7 us -> 107 us
    ppermute x0 -> x14, waiting for transfers between devices: none -> 55.1 us  [to_experts(): part = lax.ppermute(part, 'dp', [(d, d ^ mask) for d in range(ways)])]
    all_to_all x2 -> x0, waiting for transfers between devices: 37.3 us -> none  [to_experts(): lax.all_to_all(picked.reshape(experts, share, model_width), 'dp', split_a...]
    ppermute x0 -> x14, starting transfers between devices: none -> 27.7 us  [to_experts(): part = lax.ppermute(part, 'dp', [(d, d ^ mask) for d in range(ways)])]
    ppermute x46, waiting for transfers between devices: 439 us -> 420 us  [fetch(): return lax.ppermute(value, 'tensor', self._pairs(axis, shift))]
  transfers between devices with their start and end apart: 52 -> 64, of which waited for: 31 -> 34; matrix products, arithmetic and copies ran while one was open for 37% -> 36% of each run, Pallas kernels for 0% -> 0%
where the time goes in v1:
time: 1440 us; the launch traced here: 1430 us
  waiting for transfers between devices  494 us (34%)
  matrix products  356 us (25%)
  local copies, waits for them, and re-layouts  254 us (18%)
  other arithmetic  142 us (10%)
  starting transfers between devices  107 us (7%)
  blocking collectives  60.1 us (4%)
  between operations  16 us (1%)
    ppermute x46, waiting for transfers between devices, fetch(): return lax.ppermute(value, 'tensor', self._pairs(axis, shift))  420 us
    dot_general x27, matrix products, dot(): lax.dot_general(a, b, (contract, ((), ())), preferred_element_type=F32)  213 us
    ppermute x46, starting transfers between devices, fetch(): return lax.ppermute(value, 'tensor', self._pairs(axis, shift))  56.4 us
    ppermute x14, waiting for transfers between devices, to_experts(): part = lax.ppermute(part, 'dp', [(d, d ^ mask) for d in range(ways)])  55.1 us
    psum x1, blocking collectives, body(): lax.psum(norm_parts, ('dp', 'tensor'))  49.7 us
    convert_element_type x1, other arithmetic, body(): grad_scores = (attention_weights * (grad_probs - row_delta)).astype(BF16)  42.3 us
    gather x2, local copies, waits for them, and re-layouts, from_experts(): picked = every.reshape(shards * own_rows, model_width)[tok_place]  39.8 us
    dot_general x1, matrix products, body(): jnp.einsum('sqhd,skhd->shqk', grad_attended, values, preferred_element_ty...  36.9 us
  transfers between devices with their start and end apart: 64, of which 34 were waited for; matrix products, arithmetic and copies ran while one was open for 36% of the time, Pallas kernels for 0%

profile of v1, /device:TPU:0, one launch (start us, length us, event | category | flops | bytes accessed | tf_op | source)
XLA Modules:
  0.0 1427.7 jit_solution(15949260366335496869)
XLA Ops:
  46.1 19.2 %fusion = (f32[3,4,1024]{2,1,0:T(4,128)S(1)}, f32[3,4,1024,1024]{2,3,1,0:T(8,128)}) fusion(pred[3,1024,1024]{1,2,0:T(8,128)(4,1)S(1)} %broadcast_and_fusion, bf16[3,1024,4,64]{1,0,3,2:T(4,128)(2,1)S(1)} %get-tuple-element.29, bf16[3,1024,4,64]{1,0,3,2:T(4,128)(2,1)S(1)} %get-tuple-element.27), kind=kOutput, calls=%fused_computation.13 | convolution fusion | flops 1648349184 | bytes 56672256 | tf_op jit(solution)/shard_map/sqhd,skhd->shqk/dot_general | solution.py:224
  65.3 21.2 %exponential_reduce_fusion = f32[3,4,1024]{2,1,0:T(4,128)S(1)} fusion(f32[3,4,1024,1024]{2,3,1,0:T(8,128)} %get-tuple-element.70, f32[3,4,1024]{2,1,0:T(4,128)S(1)} %get-tuple-element.69, pred[3,1024,1024]{1,2,0:T(8,128)(4,1)S(1)} %broadcast_and_fusion), kind=kLoop, calls=%fused_computation.11 | loop fusion | flops 50319360 | bytes 53575680 | tf_op jit(solution)/shard_map/reduce_sum | solution.py:231
  86.5 20.1 %fusion.39 = bf16[3,1024,4,64]{1,3,2,0:T(8,128)(2,1)S(1)} fusion(bf16[3,1024,4,64]{1,0,3,2:T(4,128)(2,1)S(1)} %get-tuple-element.28, f32[3,4,1024,1024]{2,3,1,0:T(8,128)} %get-tuple-element.70, f32[3,4,1024]{2,1,0:T(4,128)S(1)} %log_add_fusion, pred[3,1024,1024]{1,2,0:T(8,128)(4,1)S(1)} %broadcast_and_fusion), kind=kOutput, calls=%fused_computation.133 | convolution fusion | flops 1661730816 | bytes 56672256 | tf_op jit(solution)/shard_map/shqk,skhd->sqhd/dot_general | solution.py:236
  122.7 19.4 %gather_fusion = pred[3072]{0:T(1024)(128)(4,1)S(1)} fusion(pred[3072]{0:T(1024)(128)(4,1)S(1)} %fusion.60, s32[3072]{0:T(1024)S(1)} %broadcast_clamp_fusion), kind=kCustom, calls=%fused_computation | custom fusion | bytes 18432 | tf_op jit(solution)/shard_map/gather | solution.py:109
  142.0 17.4 %gather_fusion.1 = s32[3072]{0:T(1024)S(1)} fusion(s32[3072]{0:T(1024)S(1)} %bitcast.249, s32[3072]{0:T(1024)S(1)} %broadcast_clamp_fusion), kind=kCustom, calls=%fused_computation.1 | custom fusion | bytes 36864 | tf_op jit(solution)/shard_map/gather | solution.py:108
  209.5 14.0 fusion.2
  256.3 17.1 %collective-permute-done.10 = bf16[1,112,1024]{2,1,0:T(8,128)(2,1)S(1)} collective-permute-done((bf16[1,112,1024]{2,1,0:T(8,128)(2,1)S(1)}, bf16[1,112,1024]{2,1,0:T(8,128)(2,1)S(1)}, u32[]{:S(2)}, u32[]{:S(2)}) %collective-permute-start.10) | collective-permute-done | bytes 229408 | tf_op jit(solution)/shard_map/ppermute | solution.py:192
  285.7 28.5 %collective-permute-done.13 = bf16[896,1024]{1,0:T(8,128)(2,1)S(1)} collective-permute-done((bf16[896,1024]{1,0:T(8,128)(2,1)S(1)}, bf16[896,1024]{1,0:T(8,128)(2,1)S(1)}, u32[]{:S(2)}, u32[]{:S(2)}) %collective-permute-start.13) | collective-permute-done | bytes 1835040 | tf_op jit(solution)/shard_map/ppermute | solution.py:35
  351.8 40.4 %collective-permute-done.16 = bf16[896,1024]{1,0:T(8,128)(2,1)S(1)} collective-permute-done((bf16[896,1024]{1,0:T(8,128)(2,1)S(1)}, bf16[896,1024]{1,0:T(8,128)(2,1)S(1)}, u32[]{:S(2)}, u32[]{:S(2)}) %collective-permute-start.16) | collective-permute-done | bytes 1835040 | tf_op jit(solution)/shard_map/ppermute | solution.py:35
  423.3 17.2 %collective-permute-done.31 = bf16[1,112,1024]{2,1,0:T(8,128)(2,1)S(1)} collective-permute-done((bf16[1,112,1024]{2,1,0:T(8,128)(2,1)S(1)}, bf16[1,112,1024]{2,1,0:T(8,128)(2,1)S(1)}, u32[]{:S(2)}, u32[]{:S(2)}) %collective-permute-start.31) | collective-permute-done | bytes 229408 | tf_op jit(solution)/shard_map/ppermute | solution.py:192
  462.6 19.6 %collective-permute-done.34 = bf16[896,1024]{1,0:T(8,128)(2,1)} collective-permute-done((bf16[896,1024]{1,0:T(8,128)(2,1)S(1)}, bf16[896,1024]{1,0:T(8,128)(2,1)}, u32[]{:S(2)}, u32[]{:S(2)}) %collective-permute-start.34) | collective-permute-done | bytes 1835040 | tf_op jit(solution)/shard_map/ppermute | solution.py:35
  547.1 16.7 %collective-permute-done.35 = bf16[896,1024]{1,0:T(8,128)(2,1)S(1)} collective-permute-done((bf16[896,1024]{1,0:T(8,128)(2,1)S(1)}, bf16[896,1024]{1,0:T(8,128)(2,1)S(1)}, u32[]{:S(2)}, u32[]{:S(2)}) %collective-permute-start.35) | collective-permute-done | bytes 1835040 | tf_op jit(solution)/shard_map/ppermute | solution.py:35
  563.8 35.9 %collective-permute-done.20 = bf16[896,1024]{1,0:T(8,128)(2,1)} collective-permute-done((bf16[896,1024]{1,0:T(8,128)(2,1)S(1)}, bf16[896,1024]{1,0:T(8,128)(2,1)}, u32[]{:S(2)}, u32[]{:S(2)}) %collective-permute-start.20) | collective-permute-done | bytes 1835040 | tf_op jit(solution)/shard_map/ppermute | solution.py:35
  606.5 37.5 %collective-permute-done.36 = bf16[896,1024]{1,0:T(8,128)(2,1)S(1)} collective-permute-done((bf16[896,1024]{1,0:T(8,128)(2,1)}, bf16[896,1024]{1,0:T(8,128)(2,1)S(1)}, u32[]{:S(2)}, u32[]{:S(2)}) %collective-permute-start.36) | collective-permute-done | bytes 1835040 | tf_op jit(solution)/shard_map/ppermute | solution.py:35
  678.0 36.6 %collective-permute-done.37 = bf16[896,1024]{1,0:T(8,128)(2,1)} collective-permute-done((bf16[896,1024]{1,0:T(8,128)(2,1)}, bf16[896,1024]{1,0:T(8,128)(2,1)}, u32[]{:S(2)}, u32[]{:S(2)}) %collective-permute-start.37) | collective-permute-done | bytes 1835040 | tf_op jit(solution)/shard_map/ppermute | solution.py:35
  723.0 18.1 %all-to-all-start = ((bf16[8,112,1024]{2,1,0:T(8,128)(2,1)}), bf16[8,112,1024]{2,1,0:T(8,128)(2,1)}, u32[]{:S(2)}, u32[]{:S(2)}) async-start(bf16[8,112,1024]{2,1,0:T(8,128)(2,1)} %bitcast.266), calls=%async_computation | async-start | bytes 3670016 | tf_op jit(solution)/shard_map/all_to_all | solution.py:197
  808.5 34.7 %collective-permute-done.57 = bf16[1024,1024]{1,0:T(8,128)(2,1)} collective-permute-done((bf16[1024,1024]{1,0:T(8,128)(2,1)}, bf16[1024,1024]{1,0:T(8,128)(2,1)}, u32[]{:S(2)}, u32[]{:S(2)}) %collective-permute-start.57) | collective-permute-done | bytes 2097184 | tf_op jit(solution)/shard_map/ppermute | solution.py:35
  888.6 13.7 collective-permute-done.22
  924.1 17.5 %collective-permute-done.39 = bf16[448,1024]{1,0:T(8,128)(2,1)S(1)} collective-permute-done((bf16[448,1024]{1,0:T(8,128)(2,1)S(1)}, bf16[448,1024]{1,0:T(8,128)(2,1)S(1)}, u32[]{:S(2)}, u32[]{:S(2)}) %collective-permute-start.39) | collective-permute-done | bytes 917536 | tf_op jit(solution)/shard_map/ppermute | solution.py:35
  952.3 16.3 %collective-permute-done.25 = bf16[448,1024]{1,0:T(8,128)(2,1)S(1)} collective-permute-done((bf16[448,1024]{1,0:T(8,128)(2,1)}, bf16[448,1024]{1,0:T(8,128)(2,1)S(1)}, u32[]{:S(2)}, u32[]{:S(2)}) %collective-permute-start.25) | collective-permute-done | bytes 917536 | tf_op jit(solution)/shard_map/ppermute | solution.py:35
  970.9 15.4 %collective-permute-done.42 = bf16[448,1024]{1,0:T(8,128)(2,1)S(1)} collective-permute-done((bf16[448,1024]{1,0:T(8,128)(2,1)S(1)}, bf16[448,1024]{1,0:T(8,128)(2,1)S(1)}, u32[]{:S(2)}, u32[]{:S(2)}) %collective-permute-start.42) | collective-permute-done | bytes 917536 | tf_op jit(solution)/shard_map/ppermute | solution.py:35
  987.3 18.8 %collective-permute-done.26 = bf16[448,1024]{1,0:T(8,128)(2,1)S(1)} collective-permute-done((bf16[448,1024]{1,0:T(8,128)(2,1)S(1)}, bf16[448,1024]{1,0:T(8,128)(2,1)S(1)}, u32[]{:S(2)}, u32[]{:S(2)}) %collective-permute-start.26) | collective-permute-done | bytes 917536 | tf_op jit(solution)/shard_map/ppermute | solution.py:35
  1006.2 19.7 %collective-permute-done.43 = bf16[448,1024]{1,0:T(8,128)(2,1)S(1)} collective-permute-done((bf16[448,1024]{1,0:T(8,128)(2,1)S(1)}, bf16[448,1024]{1,0:T(8,128)(2,1)S(1)}, u32[]{:S(2)}, u32[]{:S(2)}) %collective-permute-start.43) | collective-permute-done | bytes 917536 | tf_op jit(solution)/shard_map/ppermute | solution.py:35
  1027.2 19.9 %gather_fusion.3 = bf16[3072,1024]{1,0:T(8,128)(2,1)} fusion(bf16[3584,1024]{1,0:T(8,128)(2,1)} %bitcast.37, s32[3072]{0:T(1024)S(1)} %fusion.66), kind=kCustom, calls=%fused_computation.3 | custom fusion | bytes 12595200 | tf_op jit(solution)/shard_map/gather | solution.py:201
  1047.1 19.9 %gather_fusion.5 = bf16[3072,1024]{1,0:T(8,128)(2,1)} fusion(bf16[3584,1024]{1,0:T(8,128)(2,1)} %bitcast.51, s32[3072]{0:T(1024)S(1)} %fusion.66), kind=kCustom, calls=%fused_computation.5 | custom fusion | bytes 12595200 | tf_op jit(solution)/shard_map/gather | solution.py:201
  1067.0 17.5 %convert_add_fusion.1 = (f32[3072,1024]{1,0:T(8,128)S(1)}, bf16[3072,1024]{1,0:T(8,128)(2,1)}) fusion(bf16[3072,1024]{1,0:T(8,128)(2,1)} %param.23, bf16[3072,1024]{1,0:T(8,128)(2,1)} %gather_fusion.5, pred[3072]{0:T(1024)(128)(4,1)S(1)} %broadcast_compare_fusion, bf16[3072,1024]{1,0:T(8,128)(2,1)} %gather_fusion.3, f32[3072,1024]{1,0:T(8,128)} %get-tuple-element.72, ...), kind=kLoop, calls=%fused_computation.19 | loop fusion | flops 31457280 | bytes 56626176 | tf_op jit(solution)/shard_map/add | solution.py:287
  1098.1 36.9 %multiply_reduce_fusion = (f32[3,4,1024]{2,1,0:T(4,128)S(1)}, f32[3,4,1024,1024]{2,3,1,0:T(8,128)}) fusion(f32[3,4,1024,1024]{2,3,1,0:T(8,128)} %get-tuple-element.70, f32[3,4,1024]{2,1,0:T(4,128)S(1)} %copy-done.35, pred[3,1024,1024]{1,2,0:T(8,128)(4,1)} %copy-done.3, bf16[3,1024,4,64]{1,3,2,0:T(8,128)(2,1)S(1)} %copy.37, ...), kind=kOutput, calls=%fused_computation.9 | convolution fusion | flops 1673515008 | bytes 107053056 | tf_op jit(solution)/shard_map/sqhd,skhd->shqk/dot_general | solution.py:295
  1135.0 42.3 %multiply_convert_fusion = bf16[3,4,1024,1024]{2,3,1,0:T(8,128)(2,1)} fusion(f32[3,4,1024,1024]{2,3,1,0:T(8,128)} %get-tuple-element.82, f32[3,4,1024,1024]{2,3,1,0:T(8,128)} %get-tuple-element.70, f32[3,4,1024]{2,1,0:T(4,128)S(1)} %get-tuple-element.81, f32[3,4,1024]{2,1,0:T(4,128)S(1)} %copy-done.35, pred[3,1024,1024]{1,2,0:T(8,128)(4,1)} %copy-done.3), kind=kLoop, calls=%fused_computation.8 | loop fusion | flops 75497472 | bytes 129073152 | tf_op jit(solution)/shard_map/convert_element_type | solution.py:297
  1190.8 14.0 fusion.42
  1204.8 20.3 %fusion.40 = bf16[3,1024,4,64]{1,3,2,0:T(8,128)(2,1)S(1)} fusion(bf16[3,1024,4,64]{1,3,2,0:T(8,128)(2,1)} %copy-done.12, f32[3,4,1024,1024]{2,3,1,0:T(8,128)} %get-tuple-element.70, f32[3,4,1024]{2,1,0:T(4,128)S(1)} %copy-done.35, pred[3,1024,1024]{1,2,0:T(8,128)(4,1)} %copy-done.3), kind=kOutput, calls=%fused_computation.134 | convolution fusion | flops 1661730816 | bytes 56672256 | tf_op jit(solution)/shard_map/shqk,sqhd->skhd/dot_general | solution.py:306
  1328.0 49.7 %psum.28 = f32[2,1024]{1,0:T(2,128)S(1)} all-reduce(f32[2,1024]{1,0:T(2,128)S(1)} %pad_maximum_fusion.6), channel_id=1, replica_groups=mesh['dp'=8,'tensor'=4] {'dp','tensor'}, use_global_device_ids=true, to_apply=%region_15.16 | all-reduce | flops 2048 | bytes 16384 | tf_op jit(solution)/shard_map/psum | solution.py:328
  1399.0 16.4 %all-reduce.3.cloned.1.call-done = (f32[1024,4,192]{0,2,1:T(8,128)}, f32[4,64,1024]{2,1,0:T(8,128)}) async-done(((f32[1024,4,192]{0,2,1:T(8,128)}, f32[4,64,1024]{2,1,0:T(8,128)}), (f32[1024,4,192]{0,2,1:T(8,128)}, f32[4,64,1024]{2,1,0:T(8,128)})) %all-reduce.3.cloned.1.call-update) | async-done | bytes 4194320 | tf_op jit(solution)/shard_map/psum | solution.py:333
  (421 shorter events, 659.7 us)
Async XLA Ops:
  7.2 202.3 %all-gather.2.cloned.1.call-start = ((), (), s32[]{:S(2)}) async-start(), calls=%async_computation.2 | async-start | bytes 2621440 | tf_op jit(solution)/shard_map/all_gather | solution.py:165
  112.5 76.0 %collective-permute-start = (bf16[1536,256]{0,1:T(8,128)(2,1)}, bf16[1536,256]{0,1:T(8,128)(2,1)}, u32[]{:S(2)}, u32[]{:S(2)}) collective-permute-start(bf16[1536,256]{0,1:T(8,128)(2,1)} %get-tuple-element.60), channel_id=1, source_target_pairs={{1,0},{0,1},{3,2},{2,3},{5,4},{4,5},{7,6},{6,7},{9,8},{8,9},{11,10... | collective-permute-start | bytes 2359304 | tf_op jit(solution)/shard_map/ppermute | solution.py:35
  115.4 80.7 %collective-permute-start.2 = (bf16[1536,256]{0,1:T(8,128)(2,1)}, bf16[1536,256]{0,1:T(8,128)(2,1)}, u32[]{:S(2)}, u32[]{:S(2)}) collective-permute-start(bf16[1536,256]{0,1:T(8,128)(2,1)} %get-tuple-element.60), channel_id=1, source_target_pairs={{2,0},{3,1},{0,2},{1,3},{6,4},{7,5},{4,6},{5,7},{10,8},{11,9},{8,1... | collective-permute-start | bytes 2359304 | tf_op jit(solution)/shard_map/ppermute | solution.py:35
  116.9 77.1 %collective-permute-start.1 = (bf16[1536,256]{0,1:T(8,128)(2,1)}, bf16[1536,256]{0,1:T(8,128)(2,1)}, u32[]{:S(2)}, u32[]{:S(2)}) collective-permute-start(bf16[1536,256]{0,1:T(8,128)(2,1)} %get-tuple-element.59), channel_id=1, source_target_pairs={{1,0},{0,1},{3,2},{2,3},{5,4},{4,5},{7,6},{6,7},{9,8},{8,9},{11,10... | collective-permute-start | bytes 2359304 | tf_op jit(solution)/shard_map/ppermute | solution.py:35
  117.5 73.0 %collective-permute-start.3 = (bf16[1536,256]{0,1:T(8,128)(2,1)}, bf16[1536,256]{0,1:T(8,128)(2,1)}, u32[]{:S(2)}, u32[]{:S(2)}) collective-permute-start(bf16[1536,256]{0,1:T(8,128)(2,1)} %get-tuple-element.59), channel_id=1, source_target_pairs={{2,0},{3,1},{0,2},{1,3},{6,4},{7,5},{4,6},{5,7},{10,8},{11,9},{8,1... | collective-permute-start | bytes 2359304 | tf_op jit(solution)/shard_map/ppermute | solution.py:35
  237.1 48.5 %collective-permute-start.14 = (bf16[1024,1024]{1,0:T(8,128)(2,1)S(1)}, bf16[1024,1024]{1,0:T(8,128)(2,1)S(1)}, u32[]{:S(2)}, u32[]{:S(2)}) collective-permute-start(bf16[1024,1024]{1,0:T(8,128)(2,1)S(1)} %get-tuple-element.35), channel_id=1, source_target_pairs={{1,0},{0,1},{3,2},{2,3},{5,4},{4,5},{7,6},{6,7},{9,8},{8,9},{11,10... | collective-permute-start | bytes 6291464 | tf_op jit(solution)/shard_map/ppermute | solution.py:35
  275.2 63.6 %collective-permute-start.15 = (bf16[1024,1024]{1,0:T(8,128)(2,1)S(1)}, bf16[1024,1024]{1,0:T(8,128)(2,1)S(1)}, u32[]{:S(2)}, u32[]{:S(2)}) collective-permute-start(bf16[1024,1024]{1,0:T(8,128)(2,1)S(1)} %get-tuple-element.33), channel_id=1, source_target_pairs={{1,0},{0,1},{3,2},{2,3},{5,4},{4,5},{7,6},{6,7},{9,8},{8,9},{11,10... | collective-permute-start | bytes 6291464 | tf_op jit(solution)/shard_map/ppermute | solution.py:35
  349.2 43.0 %collective-permute-start.16 = (bf16[896,1024]{1,0:T(8,128)(2,1)S(1)}, bf16[896,1024]{1,0:T(8,128)(2,1)S(1)}, u32[]{:S(2)}, u32[]{:S(2)}) collective-permute-start(bf16[896,1024]{1,0:T(8,128)(2,1)S(1)} %split.75), channel_id=1, source_target_pairs={{2,0},{3,1},{0,2},{1,3},{6,4},{7,5},{4,6},{5,7},{10,8},{11,9},{8,1... | collective-permute-start | bytes 5505032 | tf_op jit(solution)/shard_map/ppermute | solution.py:35
  350.5 93.9 %collective-permute-start.18 = (bf16[1024,1024]{1,0:T(8,128)(2,1)S(1)}, bf16[1024,1024]{1,0:T(8,128)(2,1)}, u32[]{:S(2)}, u32[]{:S(2)}) collective-permute-start(bf16[1024,1024]{1,0:T(8,128)(2,1)S(1)} %get-tuple-element.34), channel_id=1, source_target_pairs={{2,0},{3,1},{0,2},{1,3},{6,4},{7,5},{4,6},{5,7},{10,8},{11,9},{8,1... | collective-permute-start | bytes 6291464 | tf_op jit(solution)/shard_map/ppermute | solution.py:35
  351.7 52.7 %collective-permute-start.27 = (bf16[1,112,1024]{2,1,0:T(8,128)(2,1)S(1)}, bf16[1,112,1024]{2,1,0:T(8,128)(2,1)S(1)}, u32[]{:S(2)}, u32[]{:S(2)}) collective-permute-start(bf16[1,112,1024]{2,1,0:T(8,128)(2,1)S(1)} %get-tuple-element.55), channel_id=1, source_target_pairs={{0,4},{4,0},{8,12},{12,8},{16,20},{20,16},{24,28},{28,24},{1,5},{5... | collective-permute-start | bytes 688136 | tf_op jit(solution)/shard_map/ppermute | solution.py:192
  393.4 51.1 %collective-permute-start.17 = (bf16[896,1024]{1,0:T(8,128)(2,1)S(1)}, bf16[896,1024]{1,0:T(8,128)(2,1)}, u32[]{:S(2)}, u32[]{:S(2)}) collective-permute-start(bf16[896,1024]{1,0:T(8,128)(2,1)S(1)} %fusion.43), channel_id=1, source_target_pairs={{1,0},{0,1},{3,2},{2,3},{5,4},{4,5},{7,6},{6,7},{9,8},{8,9},{11,10... | collective-permute-start | bytes 5505032 | tf_op jit(solution)/shard_map/ppermute | solution.py:35
  443.2 57.2 %collective-permute-start.19 = (bf16[1024,1024]{1,0:T(8,128)(2,1)S(1)}, bf16[1024,1024]{1,0:T(8,128)(2,1)}, u32[]{:S(2)}, u32[]{:S(2)}) collective-permute-start(bf16[1024,1024]{1,0:T(8,128)(2,1)S(1)} %get-tuple-element.32), channel_id=1, source_target_pairs={{2,0},{3,1},{0,2},{1,3},{6,4},{7,5},{4,6},{5,7},{10,8},{11,9},{8,1... | collective-permute-start | bytes 6291464 | tf_op jit(solution)/shard_map/ppermute | solution.py:35
  520.8 43.0 %collective-permute-start.35 = (bf16[896,1024]{1,0:T(8,128)(2,1)S(1)}, bf16[896,1024]{1,0:T(8,128)(2,1)S(1)}, u32[]{:S(2)}, u32[]{:S(2)}) collective-permute-start(bf16[896,1024]{1,0:T(8,128)(2,1)S(1)} %split.73), channel_id=1, source_target_pairs={{1,0},{0,1},{3,2},{2,3},{5,4},{4,5},{7,6},{6,7},{9,8},{8,9},{11,10... | collective-permute-start | bytes 5505032 | tf_op jit(solution)/shard_map/ppermute | solution.py:35
  545.5 54.2 %collective-permute-start.20 = (bf16[896,1024]{1,0:T(8,128)(2,1)S(1)}, bf16[896,1024]{1,0:T(8,128)(2,1)}, u32[]{:S(2)}, u32[]{:S(2)}) collective-permute-start(bf16[896,1024]{1,0:T(8,128)(2,1)S(1)} %split.74), channel_id=1, source_target_pairs={{1,0},{0,1},{3,2},{2,3},{5,4},{4,5},{7,6},{6,7},{9,8},{8,9},{11,10... | collective-permute-start | bytes 5505032 | tf_op jit(solution)/shard_map/ppermute | solution.py:35
  723.0 61.6 %all-to-all-start = ((bf16[8,112,1024]{2,1,0:T(8,128)(2,1)}), bf16[8,112,1024]{2,1,0:T(8,128)(2,1)}, u32[]{:S(2)}, u32[]{:S(2)}) async-start(bf16[8,112,1024]{2,1,0:T(8,128)(2,1)} %bitcast.266), calls=%async_computation | async-start | bytes 3670016 | tf_op jit(solution)/shard_map/all_to_all | solution.py:197
  749.8 48.9 %collective-permute-start.59 = (bf16[1024,1024]{1,0:T(8,128)(2,1)}, bf16[1024,1024]{1,0:T(8,128)(2,1)}, u32[]{:S(2)}, u32[]{:S(2)}) collective-permute-start(bf16[1024,1024]{1,0:T(8,128)(2,1)} %convolution_convert_fusion.1), channel_id=1, source_target_pairs={{2,0},{3,1},{0,2},{1,3},{6,4},{7,5},{4,6},{5,7},{10,8},{11,9},{8,1... | collective-permute-start | bytes 6291464 | tf_op jit(solution)/shard_map/ppermute | solution.py:35
  757.7 85.5 %collective-permute-start.57 = (bf16[1024,1024]{1,0:T(8,128)(2,1)}, bf16[1024,1024]{1,0:T(8,128)(2,1)}, u32[]{:S(2)}, u32[]{:S(2)}) collective-permute-start(bf16[1024,1024]{1,0:T(8,128)(2,1)} %convolution_convert_fusion.3), channel_id=1, source_target_pairs={{2,0},{3,1},{0,2},{1,3},{6,4},{7,5},{4,6},{5,7},{10,8},{11,9},{8,1... | collective-permute-start | bytes 6291464 | tf_op jit(solution)/shard_map/ppermute | solution.py:35
  784.6 83.8 %all-to-all-start.1 = ((bf16[8,112,1024]{2,1,0:T(8,128)(2,1)}), bf16[8,112,1024]{2,1,0:T(8,128)(2,1)}, u32[]{:S(2)}, u32[]{:S(2)}) async-start(bf16[8,112,1024]{2,1,0:T(8,128)(2,1)} %bitcast.265), calls=%async_computation.1 | async-start | bytes 3670016 | tf_op jit(solution)/shard_map/all_to_all | solution.py:197
  788.9 626.5 %all-reduce.3.cloned.1.call-start = ((), (), s32[]{:S(2)}) async-start(), calls=%async_computation.3 | async-start | bytes 8388608 | tf_op jit(solution)/shard_map/psum | solution.py:333
  870.1 51.9 %collective-permute-start.38 = (bf16[448,1024]{1,0:T(8,128)(2,1)S(1)}, bf16[448,1024]{1,0:T(8,128)(2,1)S(1)}, u32[]{:S(2)}, u32[]{:S(2)}) collective-permute-start(bf16[448,1024]{1,0:T(8,128)(2,1)S(1)} %bitcast.281), channel_id=1, source_target_pairs={{1,0},{0,1},{3,2},{2,3},{5,4},{4,5},{7,6},{6,7},{9,8},{8,9},{11,10... | collective-permute-start | bytes 2752520 | tf_op jit(solution)/shard_map/ppermute | solution.py:35
  885.2 58.6 %collective-permute-start.40 = (bf16[448,1024]{1,0:T(8,128)(2,1)S(1)}, bf16[448,1024]{1,0:T(8,128)(2,1)S(1)}, u32[]{:S(2)}, u32[]{:S(2)}) collective-permute-start(bf16[448,1024]{1,0:T(8,128)(2,1)S(1)} %bitcast.282), channel_id=1, source_target_pairs={{2,0},{3,1},{0,2},{1,3},{6,4},{7,5},{4,6},{5,7},{10,8},{11,9},{8,1... | collective-permute-start | bytes 2752520 | tf_op jit(solution)/shard_map/ppermute | solution.py:35
  905.9 43.0 %collective-permute-start.41 = (bf16[448,1024]{1,0:T(8,128)(2,1)S(1)}, bf16[448,1024]{1,0:T(8,128)(2,1)S(1)}, u32[]{:S(2)}, u32[]{:S(2)}) collective-permute-start(bf16[448,1024]{1,0:T(8,128)(2,1)S(1)} %bitcast.280), channel_id=1, source_target_pairs={{2,0},{3,1},{0,2},{1,3},{6,4},{7,5},{4,6},{5,7},{10,8},{11,9},{8,1... | collective-permute-start | bytes 2752520 | tf_op jit(solution)/shard_map/ppermute | solution.py:35
  909.6 326.9 %collective-permute-start.58 = (bf16[1024,1024]{1,0:T(8,128)(2,1)}, bf16[1024,1024]{1,0:T(8,128)(2,1)}, u32[]{:S(2)}, u32[]{:S(2)}) collective-permute-start(bf16[1024,1024]{1,0:T(8,128)(2,1)} %convolution_convert_fusion.2), channel_id=1, source_target_pairs={{1,0},{0,1},{3,2},{2,3},{5,4},{4,5},{7,6},{6,7},{9,8},{8,9},{11,10... | collective-permute-start | bytes 6291464 | tf_op jit(solution)/shard_map/ppermute | solution.py:35
  921.9 46.7 %collective-permute-start.25 = (bf16[448,1024]{1,0:T(8,128)(2,1)}, bf16[448,1024]{1,0:T(8,128)(2,1)S(1)}, u32[]{:S(2)}, u32[]{:S(2)}) collective-permute-start(bf16[448,1024]{1,0:T(8,128)(2,1)} %collective-permute-done.21), channel_id=1, source_target_pairs={{2,0},{3,1},{0,2},{1,3},{6,4},{7,5},{4,6},{5,7},{10,8},{11,9},{8,1... | collective-permute-start | bytes 2752520 | tf_op jit(solution)/shard_map/ppermute | solution.py:35
  941.6 44.8 %collective-permute-start.42 = (bf16[448,1024]{1,0:T(8,128)(2,1)S(1)}, bf16[448,1024]{1,0:T(8,128)(2,1)S(1)}, u32[]{:S(2)}, u32[]{:S(2)}) collective-permute-start(bf16[448,1024]{1,0:T(8,128)(2,1)S(1)} %collective-permute-done.38), channel_id=1, source_target_pairs={{2,0},{3,1},{0,2},{1,3},{6,4},{7,5},{4,6},{5,7},{10,8},{11,9},{8,1... | collective-permute-start | bytes 2752520 | tf_op jit(solution)/shard_map/ppermute | solution.py:35
  943.8 62.4 %collective-permute-start.26 = (bf16[448,1024]{1,0:T(8,128)(2,1)S(1)}, bf16[448,1024]{1,0:T(8,128)(2,1)S(1)}, u32[]{:S(2)}, u32[]{:S(2)}) collective-permute-start(bf16[448,1024]{1,0:T(8,128)(2,1)S(1)} %collective-permute-done.24), channel_id=1, source_target_pairs={{1,0},{0,1},{3,2},{2,3},{5,4},{4,5},{7,6},{6,7},{9,8},{8,9},{11,10... | collective-permute-start | bytes 2752520 | tf_op jit(solution)/shard_map/ppermute | solution.py:35
  948.9 76.9 %collective-permute-start.43 = (bf16[448,1024]{1,0:T(8,128)(2,1)S(1)}, bf16[448,1024]{1,0:T(8,128)(2,1)S(1)}, u32[]{:S(2)}, u32[]{:S(2)}) collective-permute-start(bf16[448,1024]{1,0:T(8,128)(2,1)S(1)} %collective-permute-done.41), channel_id=1, source_target_pairs={{1,0},{0,1},{3,2},{2,3},{5,4},{4,5},{7,6},{6,7},{9,8},{8,9},{11,10... | collective-permute-start | bytes 2752520 | tf_op jit(solution)/shard_map/ppermute | solution.py:35
  968.6 288.0 %collective-permute-start.56 = (bf16[1024,1024]{1,0:T(8,128)(2,1)}, bf16[1024,1024]{1,0:T(8,128)(2,1)}, u32[]{:S(2)}, u32[]{:S(2)}) collective-permute-start(bf16[1024,1024]{1,0:T(8,128)(2,1)} %convolution_convert_fusion.4), channel_id=1, source_target_pairs={{1,0},{0,1},{3,2},{2,3},{5,4},{4,5},{7,6},{6,7},{9,8},{8,9},{11,10... | collective-permute-start | bytes 6291464 | tf_op jit(solution)/shard_map/ppermute | solution.py:35
  1312.4 65.9 %collective-permute-start.50 = (bf16[384,1024]{1,0:T(8,128)(2,1)}, bf16[384,1024]{1,0:T(8,128)(2,1)S(1)}, u32[]{:S(2)}, u32[]{:S(2)}) collective-permute-start(bf16[384,1024]{1,0:T(8,128)(2,1)} %get-tuple-element.58), channel_id=1, source_target_pairs={{1,0},{0,1},{3,2},{2,3},{5,4},{4,5},{7,6},{6,7},{9,8},{8,9},{11,10... | collective-permute-start | bytes 2359304 | tf_op jit(solution)/shard_map/ppermute | solution.py:35
  1313.1 67.5 %collective-permute-start.53 = (bf16[384,1024]{1,0:T(8,128)(2,1)}, bf16[384,1024]{1,0:T(8,128)(2,1)S(1)}, u32[]{:S(2)}, u32[]{:S(2)}) collective-permute-start(bf16[384,1024]{1,0:T(8,128)(2,1)} %get-tuple-element.57), channel_id=1, source_target_pairs={{2,0},{3,1},{0,2},{1,3},{6,4},{7,5},{4,6},{5,7},{10,8},{11,9},{8,1... | collective-permute-start | bytes 2359304 | tf_op jit(solution)/shard_map/ppermute | solution.py:35
  1317.2 65.1 %collective-permute-start.51 = (bf16[384,1024]{1,0:T(8,128)(2,1)}, bf16[384,1024]{1,0:T(8,128)(2,1)}, u32[]{:S(2)}, u32[]{:S(2)}) collective-permute-start(bf16[384,1024]{1,0:T(8,128)(2,1)} %get-tuple-element.57), channel_id=1, source_target_pairs={{1,0},{0,1},{3,2},{2,3},{5,4},{4,5},{7,6},{6,7},{9,8},{8,9},{11,10... | collective-permute-start | bytes 2359304 | tf_op jit(solution)/shard_map/ppermute | solution.py:35
  1318.6 65.7 %collective-permute-start.52 = (bf16[384,1024]{1,0:T(8,128)(2,1)}, bf16[384,1024]{1,0:T(8,128)(2,1)}, u32[]{:S(2)}, u32[]{:S(2)}) collective-permute-start(bf16[384,1024]{1,0:T(8,128)(2,1)} %get-tuple-element.58), channel_id=1, source_target_pairs={{2,0},{3,1},{0,2},{1,3},{6,4},{7,5},{4,6},{5,7},{10,8},{11,9},{8,1... | collective-permute-start | bytes 2359304 | tf_op jit(solution)/shard_map/ppermute | solution.py:35
  (105 other events, 2814.6 us)
Sparse Core Ops, SparseCore 0:
  117.6 50.9 all-gather.1
  1317.3 98.1 all-reduce.2
